TPU v7x, 512 devices: a whole 4x4x16 slice. The times are simulated.
512 devices in a mesh: gx: 8 (over y, core), gy: 16 (over x, z_lo), gz: 4 (over z_hi).
Axes of the slice: x: 4, y: 4, z: 16 (z_hi: 4, z_lo: 4; z = z_hi * 4 + z_lo), core: 2. Of those that a mesh axis runs over, the one named last changes fastest.
Arguments:
- right_side: float32 [8, 16, 4, 64, 512], P('gx', 'gy', 'gz'), may hold values from -6 to 6
- diag_blocks: float32 [4, 64, 64], replicated, may hold values from -0.27 to 17.9, as said below
- face_blocks: float32 [6, 4, 64, 64], replicated, may hold values from -2.42 to 0.22
- prolong: float32 [8, 64, 64], replicated, may hold values from -0.75 to 0.75
- mats_fine: int32 [8, 16, 4, 512], P('gx', 'gy', 'gz'), may hold values from 0 to 3
- mats_mid: int32 [8, 16, 4, 64], P('gx', 'gy', 'gz'), may hold values from 0 to 3
- mats_coarse: int32 [8, 16, 4, 8], P('gx', 'gy', 'gz'), may hold values from 0 to 3
Outputs:
- solution: float32 [8, 16, 4, 64, 512], P('gx', 'gy', 'gz')
Inputs may be any that keep to these rules, and one draw needn't show every extreme that they name: `diag_blocks`: each block is symmetric positive definite.
All inputs are finite; a program needn't handle non-finite values.
Results may differ from a plain program's by a relative error of at most 0.0003.
Values sent between devices are 32-bit elements; how exact they have to be, the bound alone decides.
A program may use at most 64 MiB of HBM per device.

v0:
```python
from functools import partial

import jax
import jax.numpy as jnp
from jax import lax
from jax.sharding import PartitionSpec as P

MODES = 64
MATERIALS = 4
SWEEPS = 2
COARSE_SWEEPS = 4
CYCLES = 2
CX = 8
CY = 8
CZ = 8


relax_weight = 0.7
restrict_scale = 0.6
highest = lax.Precision.HIGHEST


def padded_2(shard, sides, width):
    for axis, dim in sides:
        size, length = (lax.axis_size(axis), shard.shape[dim])
        up = [(i, (i + 1) % size) for i in range(size - 1)]
        down = [(j, i) for i, j in up]
        last = lax.slice_in_dim(shard, length - width, length, axis=dim)
        first = lax.slice_in_dim(shard, 0, width, axis=dim)
        before = lax.ppermute(last, axis, up)
        after = lax.ppermute(first, axis, down)
        shard = jnp.concatenate([before, shard, after], axis=dim)
    return shard


def inverse_blocks(diag_blocks):
    identity = jnp.eye(MODES, dtype=diag_blocks.dtype)
    result = []
    for material in range(MATERIALS):
        factor = jnp.linalg.cholesky(diag_blocks[material])
        result.append(jax.scipy.linalg.cho_solve((factor, True), identity))
    return jnp.stack(result).reshape(MATERIALS * MODES, MODES)


def coupling_matrix(diag_blocks, face_blocks):
    blocks = jnp.concatenate([diag_blocks[None], face_blocks], axis=0)
    return jnp.transpose(blocks, (1, 2, 0, 3)).reshape(MATERIALS * MODES, 7 * MODES)


def choose_blocks(weights, columns, onehot):
    product = jnp.dot(weights, columns, precision=highest, preferred_element_type=jnp.float32)
    product = product.reshape(MATERIALS, MODES, columns.shape[1])
    return jnp.sum(product * onehot.reshape(MATERIALS, 1, columns.shape[1]), axis=0)


def operate(padded, onehot, coupling):
    centre = padded[:, 1:-1, 1:-1, 1:-1]
    stacked = jnp.concatenate(
        [
            centre,
            padded[:, 2:, 1:-1, 1:-1],
            padded[:, :-2, 1:-1, 1:-1],
            padded[:, 1:-1, 2:, 1:-1],
            padded[:, 1:-1, :-2, 1:-1],
            padded[:, 1:-1, 1:-1, 2:],
            padded[:, 1:-1, 1:-1, :-2],
        ],
        axis=0,
    )
    columns = stacked.reshape(7 * MODES, -1)
    return choose_blocks(coupling, columns, onehot.reshape(MATERIALS, -1)).reshape(centre.shape)


def apply_inverse(inverse, field, onehot):
    return choose_blocks(inverse, field.reshape(MODES, -1), onehot.reshape(MATERIALS, -1)).reshape(
        field.shape
    )


def restrict(field, prolong):
    blocked = field.reshape(
        MODES, field.shape[1] // 2, 2, field.shape[2] // 2, 2, field.shape[3] // 2, 2
    )
    return restrict_scale * jnp.einsum(
        "abcji,jxaybzc->ixyz", prolong.reshape(2, 2, 2, MODES, MODES), blocked, precision=highest
    )


def expand(coarse_field, prolong):
    finer = jnp.einsum(
        "abcji,ixyz->jxaybzc",
        prolong.reshape(2, 2, 2, MODES, MODES),
        coarse_field,
        precision=highest,
    )
    return finer.reshape(
        MODES, 2 * coarse_field.shape[1], 2 * coarse_field.shape[2], 2 * coarse_field.shape[3]
    )


def make_onehot(materials):
    return (materials[None] == jnp.arange(MATERIALS, dtype=jnp.int32)[:, None, None, None]).astype(
        jnp.float32
    )


def fine_border(field):
    return padded_2(field, (("gx", 1), ("gy", 2), ("gz", 3)), 1)


def coarse_border(field):
    return padded_2(field, (("gx", 1), ("gy", 2), ("gz", 3)), 1)


def smooth(iterate, source, onehot, border, inverse, coupling):
    residual = source - operate(border(iterate), onehot, coupling)
    return iterate + relax_weight * apply_inverse(inverse, residual, onehot)


def coarse_solve(source, onehot, border, inverse, coupling):
    iterate = relax_weight * apply_inverse(inverse, source, onehot)
    for repeat in range(COARSE_SWEEPS - 1):
        iterate = smooth(iterate, source, onehot, border, inverse, coupling)
    return iterate


def middle_cycle(source, onehot, border, inverse, coupling, prolong, coarse_solver):
    iterate = relax_weight * apply_inverse(inverse, source, onehot)
    iterate = smooth(iterate, source, onehot, border, inverse, coupling)
    residual = source - operate(border(iterate), onehot, coupling)
    iterate = iterate + expand(coarse_solver(restrict(residual, prolong)), prolong)
    for repeat in range(SWEEPS):
        iterate = smooth(iterate, source, onehot, border, inverse, coupling)
    return iterate


def single_steps(iterate, actions, source, onehot, inverse, coupling):
    residual = None
    for action in actions:
        if action == "sweep":
            iterate = smooth(iterate, source, onehot, fine_border, inverse, coupling)
        else:
            residual = source - operate(fine_border(iterate), onehot, coupling)
    return (iterate, residual)


def per_device(right_side, diag_blocks, face_blocks, prolong, mats_fine, mats_mid, mats_coarse):
    inverse = inverse_blocks(diag_blocks)
    coupling = coupling_matrix(diag_blocks, face_blocks)
    source = right_side[0, 0, 0].reshape(MODES, CX, CY, CZ)
    onehot_fine = make_onehot(mats_fine[0, 0, 0].reshape(CX, CY, CZ))
    onehot_mid = make_onehot(mats_mid[0, 0, 0].reshape(CX // 2, CY // 2, CZ // 2))
    onehot_coarse = make_onehot(mats_coarse[0, 0, 0].reshape(CX // 4, CY // 4, CZ // 4))
    stepper = partial(
        single_steps, source=source, onehot=onehot_fine, inverse=inverse, coupling=coupling
    )

    def spread(coarse_source):
        return coarse_solve(coarse_source, onehot_coarse, coarse_border, inverse, coupling)

    iterate = relax_weight * apply_inverse(inverse, source, onehot_fine)
    for cycle_index in range(CYCLES):
        if cycle_index == 0:
            actions = ["sweep"] * (SWEEPS - 1) + ["residual"]
        else:
            actions = ["sweep"] * SWEEPS + ["residual"]
        iterate, residual = stepper(iterate, actions)
        iterate = iterate + expand(
            middle_cycle(
                restrict(residual, prolong),
                onehot_mid,
                coarse_border,
                inverse,
                coupling,
                prolong,
                spread,
            ),
            prolong,
        )
        iterate, unused_residual = stepper(iterate, ["sweep"] * SWEEPS)
    return iterate.reshape(MODES, CX * CY * CZ)[None, None, None]


def solution(mesh):
    placed = (
        P("gx", "gy", "gz", None, None),
        P(),
        P(),
        P(),
        P("gx", "gy", "gz", None),
        P("gx", "gy", "gz", None),
        P("gx", "gy", "gz", None),
    )
    return jax.shard_map(
        per_device,
        mesh=mesh,
        in_specs=placed,
        out_specs=P("gx", "gy", "gz", None, None),
        check_vma=False,
    )
```

profile of v0, /device:TPU:97, one launch (start us, length us, event | category | flops | bytes accessed | tf_op | source)
XLA Modules:
  0.0 818.1 jit_solution(15418661582877436803)
XLA Ops:
  72.7 8.8 %collective-permute-start.5 = (f32[64,10,10,1]{0,3,2,1:T(1,128)S(1)}, f32[64,10,10,1]{0,3,2,1:T(1,128)S(1)}, u32[]{:S(2)}, u32[]{:S(2)}) collective-permute-start(f32[64,10,10,1]{0,3,2,1:T(1,128)S(1)} %get-tuple-element.41), channel_id=1, source_target_pairs={{0,1},{1,2},{2,3},{4,5},{5,6},{6,7},{8,9},{9,10},{10,11},{12,13},{... | collective-permute-start | bytes 76808 | tf_op jit(solution)/shard_map/ppermute | solution.py:30
  83.8 10.6 %collective-permute-done.4 = f32[64,10,10,1]{0,3,2,1:T(1,128)S(1)} collective-permute-done((f32[64,10,10,1]{0,3,2,1:T(1,128)S(1)}, f32[64,10,10,1]{0,3,2,1:T(1,128)S(1)}, u32[]{:S(2)}, u32[]{:S(2)}) %collective-permute-start.4) | collective-permute-done | bytes 25632 | tf_op jit(solution)/shard_map/ppermute | solution.py:31
  125.0 8.2 %collective-permute-done.10 = f32[64,10,10,1]{0,3,2,1:T(1,128)S(1)} collective-permute-done((f32[64,10,10,1]{0,3,2,1:T(1,128)S(1)}, f32[64,10,10,1]{0,3,2,1:T(1,128)S(1)}, u32[]{:S(2)}, u32[]{:S(2)}) %collective-permute-start.10) | collective-permute-done | bytes 25632 | tf_op jit(solution)/shard_map/ppermute | solution.py:31
  162.6 7.1 collective-permute-done.16
  193.6 7.6 collective-permute-done.22
  223.9 7.3 collective-permute-done.28
  253.6 7.3 collective-permute-done.34
  283.6 7.1 collective-permute-done.40
  314.1 7.6 collective-permute-done.46
  344.2 7.6 collective-permute-done.52
  376.4 7.4 collective-permute-done.58
  411.7 7.4 collective-permute-done.64
  448.3 8.0 collective-permute-done.70
  484.3 8.2 %collective-permute-done.76 = f32[64,10,10,1]{0,3,2,1:T(1,128)S(1)} collective-permute-done((f32[64,10,10,1]{0,3,2,1:T(1,128)S(1)}, f32[64,10,10,1]{0,3,2,1:T(1,128)S(1)}, u32[]{:S(2)}, u32[]{:S(2)}) %collective-permute-start.76) | collective-permute-done | bytes 25632 | tf_op jit(solution)/shard_map/ppermute | solution.py:31
  520.5 8.2 %collective-permute-done.82 = f32[64,10,10,1]{0,3,2,1:T(1,128)S(1)} collective-permute-done((f32[64,10,10,1]{0,3,2,1:T(1,128)S(1)}, f32[64,10,10,1]{0,3,2,1:T(1,128)S(1)}, u32[]{:S(2)}, u32[]{:S(2)}) %collective-permute-start.82) | collective-permute-done | bytes 25632 | tf_op jit(solution)/shard_map/ppermute | solution.py:31
  555.5 7.1 collective-permute-done.88
  585.9 7.6 collective-permute-done.94
  616.1 7.3 collective-permute-done.100
  645.9 7.3 collective-permute-done.106
  675.7 7.3 collective-permute-done.112
  706.4 7.6 collective-permute-done.118
  736.5 7.6 collective-permute-done.124
  768.6 7.4 collective-permute-done.130
  804.2 8.1 collective-permute-done.136
  (647 shorter events, 628.6 us)
Async XLA Ops:
  72.7 11.1 %collective-permute-start.5 = (f32[64,10,10,1]{0,3,2,1:T(1,128)S(1)}, f32[64,10,10,1]{0,3,2,1:T(1,128)S(1)}, u32[]{:S(2)}, u32[]{:S(2)}) collective-permute-start(f32[64,10,10,1]{0,3,2,1:T(1,128)S(1)} %get-tuple-element.41), channel_id=1, source_target_pairs={{0,1},{1,2},{2,3},{4,5},{5,6},{6,7},{8,9},{9,10},{10,11},{12,13},{... | collective-permute-start | bytes 76808 | tf_op jit(solution)/shard_map/ppermute | solution.py:30
  81.5 12.9 %collective-permute-start.4 = (f32[64,10,10,1]{0,3,2,1:T(1,128)S(1)}, f32[64,10,10,1]{0,3,2,1:T(1,128)S(1)}, u32[]{:S(2)}, u32[]{:S(2)}) collective-permute-start(f32[64,10,10,1]{0,3,2,1:T(1,128)S(1)} %get-tuple-element.42), channel_id=1, source_target_pairs={{1,0},{2,1},{3,2},{5,4},{6,5},{7,6},{9,8},{10,9},{11,10},{13,12},{... | collective-permute-start | bytes 76808 | tf_op jit(solution)/shard_map/ppermute | solution.py:31
  123.6 9.6 %collective-permute-start.10 = (f32[64,10,10,1]{0,3,2,1:T(1,128)S(1)}, f32[64,10,10,1]{0,3,2,1:T(1,128)S(1)}, u32[]{:S(2)}, u32[]{:S(2)}) collective-permute-start(f32[64,10,10,1]{0,3,2,1:T(1,128)S(1)} %get-tuple-element.38), channel_id=1, source_target_pairs={{1,0},{2,1},{3,2},{5,4},{6,5},{7,6},{9,8},{10,9},{11,10},{13,12},{... | collective-permute-start | bytes 76808 | tf_op jit(solution)/shard_map/ppermute | solution.py:31
  161.3 8.4 %collective-permute-start.16 = (f32[64,6,6,1]{0,3,2,1:T(1,128)S(1)}, f32[64,6,6,1]{0,3,2,1:T(1,128)S(1)}, u32[]{:S(2)}, u32[]{:S(2)}) collective-permute-start(f32[64,6,6,1]{0,3,2,1:T(1,128)S(1)} %get-tuple-element.154), channel_id=1, source_target_pairs={{1,0},{2,1},{3,2},{5,4},{6,5},{7,6},{9,8},{10,9},{11,10},{13,12},{... | collective-permute-start | bytes 27656 | tf_op jit(solution)/shard_map/ppermute | solution.py:31
  192.3 8.9 %collective-permute-start.22 = (f32[64,6,6,1]{0,3,2,1:T(1,128)S(1)}, f32[64,6,6,1]{0,3,2,1:T(1,128)S(1)}, u32[]{:S(2)}, u32[]{:S(2)}) collective-permute-start(f32[64,6,6,1]{0,3,2,1:T(1,128)S(1)} %get-tuple-element.150), channel_id=1, source_target_pairs={{1,0},{2,1},{3,2},{5,4},{6,5},{7,6},{9,8},{10,9},{11,10},{13,12},{... | collective-permute-start | bytes 27656 | tf_op jit(solution)/shard_map/ppermute | solution.py:31
  222.5 8.6 %collective-permute-start.28 = (f32[64,4,4,1]{0,3,2,1:T(1,128)S(1)}, f32[64,4,4,1]{0,3,2,1:T(1,128)S(1)}, u32[]{:S(2)}, u32[]{:S(2)}) collective-permute-start(f32[64,4,4,1]{0,3,2,1:T(1,128)S(1)} %get-tuple-element.246), channel_id=1, source_target_pairs={{1,0},{2,1},{3,2},{5,4},{6,5},{7,6},{9,8},{10,9},{11,10},{13,12},{... | collective-permute-start | bytes 12296 | tf_op jit(solution)/shard_map/ppermute | solution.py:31
  252.3 8.6 %collective-permute-start.34 = (f32[64,4,4,1]{0,3,2,1:T(1,128)S(1)}, f32[64,4,4,1]{0,3,2,1:T(1,128)S(1)}, u32[]{:S(2)}, u32[]{:S(2)}) collective-permute-start(f32[64,4,4,1]{0,3,2,1:T(1,128)S(1)} %get-tuple-element.242), channel_id=1, source_target_pairs={{1,0},{2,1},{3,2},{5,4},{6,5},{7,6},{9,8},{10,9},{11,10},{13,12},{... | collective-permute-start | bytes 12296 | tf_op jit(solution)/shard_map/ppermute | solution.py:31
  282.1 8.6 %collective-permute-start.40 = (f32[64,4,4,1]{0,3,2,1:T(1,128)S(1)}, f32[64,4,4,1]{0,3,2,1:T(1,128)S(1)}, u32[]{:S(2)}, u32[]{:S(2)}) collective-permute-start(f32[64,4,4,1]{0,3,2,1:T(1,128)S(1)} %get-tuple-element.238), channel_id=1, source_target_pairs={{1,0},{2,1},{3,2},{5,4},{6,5},{7,6},{9,8},{10,9},{11,10},{13,12},{... | collective-permute-start | bytes 12296 | tf_op jit(solution)/shard_map/ppermute | solution.py:31
  312.8 8.9 %collective-permute-start.46 = (f32[64,6,6,1]{0,3,2,1:T(1,128)S(1)}, f32[64,6,6,1]{0,3,2,1:T(1,128)S(1)}, u32[]{:S(2)}, u32[]{:S(2)}) collective-permute-start(f32[64,6,6,1]{0,3,2,1:T(1,128)S(1)} %get-tuple-element.146), channel_id=1, source_target_pairs={{1,0},{2,1},{3,2},{5,4},{6,5},{7,6},{9,8},{10,9},{11,10},{13,12},{... | collective-permute-start | bytes 27656 | tf_op jit(solution)/shard_map/ppermute | solution.py:31
  342.9 8.9 %collective-permute-start.52 = (f32[64,6,6,1]{0,3,2,1:T(1,128)S(1)}, f32[64,6,6,1]{0,3,2,1:T(1,128)S(1)}, u32[]{:S(2)}, u32[]{:S(2)}) collective-permute-start(f32[64,6,6,1]{0,3,2,1:T(1,128)S(1)} %get-tuple-element.142), channel_id=1, source_target_pairs={{1,0},{2,1},{3,2},{5,4},{6,5},{7,6},{9,8},{10,9},{11,10},{13,12},{... | collective-permute-start | bytes 27656 | tf_op jit(solution)/shard_map/ppermute | solution.py:31
  374.7 9.1 %collective-permute-start.58 = (f32[64,10,10,1]{0,3,2,1:T(1,128)S(1)}, f32[64,10,10,1]{0,3,2,1:T(1,128)S(1)}, u32[]{:S(2)}, u32[]{:S(2)}) collective-permute-start(f32[64,10,10,1]{0,3,2,1:T(1,128)S(1)} %get-tuple-element.34), channel_id=1, source_target_pairs={{1,0},{2,1},{3,2},{5,4},{6,5},{7,6},{9,8},{10,9},{11,10},{13,12},{... | collective-permute-start | bytes 76808 | tf_op jit(solution)/shard_map/ppermute | solution.py:31
  410.0 9.1 %collective-permute-start.64 = (f32[64,10,10,1]{0,3,2,1:T(1,128)S(1)}, f32[64,10,10,1]{0,3,2,1:T(1,128)S(1)}, u32[]{:S(2)}, u32[]{:S(2)}) collective-permute-start(f32[64,10,10,1]{0,3,2,1:T(1,128)S(1)} %get-tuple-element.30), channel_id=1, source_target_pairs={{1,0},{2,1},{3,2},{5,4},{6,5},{7,6},{9,8},{10,9},{11,10},{13,12},{... | collective-permute-start | bytes 76808 | tf_op jit(solution)/shard_map/ppermute | solution.py:31
  446.8 9.6 %collective-permute-start.70 = (f32[64,10,10,1]{0,3,2,1:T(1,128)S(1)}, f32[64,10,10,1]{0,3,2,1:T(1,128)S(1)}, u32[]{:S(2)}, u32[]{:S(2)}) collective-permute-start(f32[64,10,10,1]{0,3,2,1:T(1,128)S(1)} %get-tuple-element.26), channel_id=1, source_target_pairs={{1,0},{2,1},{3,2},{5,4},{6,5},{7,6},{9,8},{10,9},{11,10},{13,12},{... | collective-permute-start | bytes 76808 | tf_op jit(solution)/shard_map/ppermute | solution.py:31
  482.9 9.6 %collective-permute-start.76 = (f32[64,10,10,1]{0,3,2,1:T(1,128)S(1)}, f32[64,10,10,1]{0,3,2,1:T(1,128)S(1)}, u32[]{:S(2)}, u32[]{:S(2)}) collective-permute-start(f32[64,10,10,1]{0,3,2,1:T(1,128)S(1)} %get-tuple-element.22), channel_id=1, source_target_pairs={{1,0},{2,1},{3,2},{5,4},{6,5},{7,6},{9,8},{10,9},{11,10},{13,12},{... | collective-permute-start | bytes 76808 | tf_op jit(solution)/shard_map/ppermute | solution.py:31
  519.2 9.6 %collective-permute-start.82 = (f32[64,10,10,1]{0,3,2,1:T(1,128)S(1)}, f32[64,10,10,1]{0,3,2,1:T(1,128)S(1)}, u32[]{:S(2)}, u32[]{:S(2)}) collective-permute-start(f32[64,10,10,1]{0,3,2,1:T(1,128)S(1)} %get-tuple-element.18), channel_id=1, source_target_pairs={{1,0},{2,1},{3,2},{5,4},{6,5},{7,6},{9,8},{10,9},{11,10},{13,12},{... | collective-permute-start | bytes 76808 | tf_op jit(solution)/shard_map/ppermute | solution.py:31
  554.2 8.4 %collective-permute-start.88 = (f32[64,6,6,1]{0,3,2,1:T(1,128)S(1)}, f32[64,6,6,1]{0,3,2,1:T(1,128)S(1)}, u32[]{:S(2)}, u32[]{:S(2)}) collective-permute-start(f32[64,6,6,1]{0,3,2,1:T(1,128)S(1)} %get-tuple-element.138), channel_id=1, source_target_pairs={{1,0},{2,1},{3,2},{5,4},{6,5},{7,6},{9,8},{10,9},{11,10},{13,12},{... | collective-permute-start | bytes 27656 | tf_op jit(solution)/shard_map/ppermute | solution.py:31
  584.5 8.9 %collective-permute-start.94 = (f32[64,6,6,1]{0,3,2,1:T(1,128)S(1)}, f32[64,6,6,1]{0,3,2,1:T(1,128)S(1)}, u32[]{:S(2)}, u32[]{:S(2)}) collective-permute-start(f32[64,6,6,1]{0,3,2,1:T(1,128)S(1)} %get-tuple-element.134), channel_id=1, source_target_pairs={{1,0},{2,1},{3,2},{5,4},{6,5},{7,6},{9,8},{10,9},{11,10},{13,12},{... | collective-permute-start | bytes 27656 | tf_op jit(solution)/shard_map/ppermute | solution.py:31
  614.8 8.6 %collective-permute-start.100 = (f32[64,4,4,1]{0,3,2,1:T(1,128)S(1)}, f32[64,4,4,1]{0,3,2,1:T(1,128)S(1)}, u32[]{:S(2)}, u32[]{:S(2)}) collective-permute-start(f32[64,4,4,1]{0,3,2,1:T(1,128)S(1)} %get-tuple-element.234), channel_id=1, source_target_pairs={{1,0},{2,1},{3,2},{5,4},{6,5},{7,6},{9,8},{10,9},{11,10},{13,12},{... | collective-permute-start | bytes 12296 | tf_op jit(solution)/shard_map/ppermute | solution.py:31
  644.6 8.6 %collective-permute-start.106 = (f32[64,4,4,1]{0,3,2,1:T(1,128)S(1)}, f32[64,4,4,1]{0,3,2,1:T(1,128)S(1)}, u32[]{:S(2)}, u32[]{:S(2)}) collective-permute-start(f32[64,4,4,1]{0,3,2,1:T(1,128)S(1)} %get-tuple-element.230), channel_id=1, source_target_pairs={{1,0},{2,1},{3,2},{5,4},{6,5},{7,6},{9,8},{10,9},{11,10},{13,12},{... | collective-permute-start | bytes 12296 | tf_op jit(solution)/shard_map/ppermute | solution.py:31
  674.4 8.6 %collective-permute-start.112 = (f32[64,4,4,1]{0,3,2,1:T(1,128)S(1)}, f32[64,4,4,1]{0,3,2,1:T(1,128)S(1)}, u32[]{:S(2)}, u32[]{:S(2)}) collective-permute-start(f32[64,4,4,1]{0,3,2,1:T(1,128)S(1)} %get-tuple-element.226), channel_id=1, source_target_pairs={{1,0},{2,1},{3,2},{5,4},{6,5},{7,6},{9,8},{10,9},{11,10},{13,12},{... | collective-permute-start | bytes 12296 | tf_op jit(solution)/shard_map/ppermute | solution.py:31
  705.1 8.9 %collective-permute-start.118 = (f32[64,6,6,1]{0,3,2,1:T(1,128)S(1)}, f32[64,6,6,1]{0,3,2,1:T(1,128)S(1)}, u32[]{:S(2)}, u32[]{:S(2)}) collective-permute-start(f32[64,6,6,1]{0,3,2,1:T(1,128)S(1)} %get-tuple-element.130), channel_id=1, source_target_pairs={{1,0},{2,1},{3,2},{5,4},{6,5},{7,6},{9,8},{10,9},{11,10},{13,12},{... | collective-permute-start | bytes 27656 | tf_op jit(solution)/shard_map/ppermute | solution.py:31
  735.1 8.9 %collective-permute-start.124 = (f32[64,6,6,1]{0,3,2,1:T(1,128)S(1)}, f32[64,6,6,1]{0,3,2,1:T(1,128)S(1)}, u32[]{:S(2)}, u32[]{:S(2)}) collective-permute-start(f32[64,6,6,1]{0,3,2,1:T(1,128)S(1)} %get-tuple-element.126), channel_id=1, source_target_pairs={{1,0},{2,1},{3,2},{5,4},{6,5},{7,6},{9,8},{10,9},{11,10},{13,12},{... | collective-permute-start | bytes 27656 | tf_op jit(solution)/shard_map/ppermute | solution.py:31
  766.9 9.1 %collective-permute-start.130 = (f32[64,10,10,1]{0,3,2,1:T(1,128)S(1)}, f32[64,10,10,1]{0,3,2,1:T(1,128)S(1)}, u32[]{:S(2)}, u32[]{:S(2)}) collective-permute-start(f32[64,10,10,1]{0,3,2,1:T(1,128)S(1)} %get-tuple-element.14), channel_id=1, source_target_pairs={{1,0},{2,1},{3,2},{5,4},{6,5},{7,6},{9,8},{10,9},{11,10},{13,12},{... | collective-permute-start | bytes 76808 | tf_op jit(solution)/shard_map/ppermute | solution.py:31
  802.8 9.4 %collective-permute-start.136 = (f32[64,10,10,1]{0,3,2,1:T(1,128)S(1)}, f32[64,10,10,1]{0,3,2,1:T(1,128)S(1)}, u32[]{:S(2)}, u32[]{:S(2)}) collective-permute-start(f32[64,10,10,1]{0,3,2,1:T(1,128)S(1)} %get-tuple-element.10), channel_id=1, source_target_pairs={{1,0},{2,1},{3,2},{5,4},{6,5},{7,6},{9,8},{10,9},{11,10},{13,12},{... | collective-permute-start | bytes 76808 | tf_op jit(solution)/shard_map/ppermute | solution.py:31
  (134 other events, 802.2 us)
where the time goes:
time: 830 us; the launch traced here: 818 us
  starting transfers between devices  348 us (42%)
  waiting for transfers between devices  339 us (41%)
  other arithmetic  62.7 us (8%)
  matrix products  35.1 us (4%)
  local copies, waits for them, and re-layouts  28.7 us (3%)
    ppermute x69, waiting for transfers between devices, padded_2(): after = lax.ppermute(first, axis, down)  338 us
    ppermute x69, starting transfers between devices, padded_2(): before = lax.ppermute(last, axis, up)  199 us
    ppermute x69, starting transfers between devices, padded_2(): after = lax.ppermute(first, axis, down)  149 us
    dot_general x47, matrix products, choose_blocks(): jnp.dot(weights, columns, precision=highest, preferred_element_type=jnp.f...  28.3 us
    another operation x12, other arithmetic, inverse_blocks(): factor = jnp.linalg.cholesky(diag_blocks[material])  26.1 us
    another operation x8, other arithmetic, inverse_blocks(): result.append(jax.scipy.linalg.cho_solve((factor, True), identity))  22.2 us
  transfers between devices with their start and end apart: 138, of which 73 were waited for; matrix products, arithmetic and copies ran while one was open for 0% of the time, Pallas kernels for 0%

commit v1 on v0

v1 whole, which is shorter than its diff:
```python
from functools import partial

import jax
import jax.numpy as jnp
from jax import lax
from jax.experimental import pallas as pl
from jax.experimental.pallas import tpu as pltpu
from jax.sharding import PartitionSpec as P

MODES = 64
MATERIALS = 4
SWEEPS = 2
COARSE_SWEEPS = 4
CYCLES = 2
ROWS = (512, 64, 8)
TILE_DIMS = ((2, 2, 2, 2, 2, 2), (2, 2, 2), ())
FACE_ROWS = (32, 8, 8)
AXES = ("gx", "gy", "gz")
WEIGHT = 0.7
SCALE = 0.6
SUB = (4, 2, 1)
f32 = jnp.float32
bf16 = jnp.bfloat16
highest = lax.Precision.HIGHEST


def lanes(rows):
    return lax.broadcasted_iota(jnp.int32, (rows, 128), 1)


def swap_halves(x):
    return pltpu.roll(x, 64, axis=1)


def split(x):
    high = x.astype(bf16).astype(f32)
    return jnp.where(lanes(x.shape[0]) < 64, high, x - high)


def bit_is(dim, value):
    sub = lax.broadcasted_iota(jnp.int32, (8, 128), 0)
    return (jnp.right_shift(sub, 2 - dim) & 1) == value


def roll_sub(x, amount):
    shape = x.shape
    return pltpu.roll(x.reshape(-1, 8, 128), (-amount) % 8, axis=1).reshape(shape)


def pair(weights):
    high = weights.astype(bf16)
    return high, (weights - high.astype(f32)).astype(bf16)


def chosen(product, material):
    rows = product.shape[0]
    half = jnp.where(lanes(rows) < 64, 0.0, 1.0)
    offset = material - half
    kept = jnp.where(offset == 0.0, product[:, :128], jnp.where(offset == 2.0, product[:, 128:], 0.0))
    return kept + swap_halves(kept)


def twice(x, w_ref):
    return jnp.dot(jnp.concatenate([x, x], axis=1), w_ref[...], preferred_element_type=f32)


def three(x):
    a = x.astype(bf16)
    rest = x - a.astype(f32)
    b = rest.astype(bf16)
    return a, b, (rest - b.astype(f32)).astype(bf16)


def element_of_row(row):
    def bit(n):
        return jnp.right_shift(row, n) & 1
    x = bit(8) + 2 * bit(5) + 4 * bit(2)
    y = bit(7) + 2 * bit(4) + 4 * bit(1)
    z = bit(6) + 2 * bit(3) + 4 * bit(0)
    return x * 64 + y * 8 + z


def middle_of_row(row):
    def bit(n):
        return jnp.right_shift(row, n) & 1
    x = bit(5) + 2 * bit(2)
    y = bit(4) + 2 * bit(1)
    z = bit(3) + 2 * bit(0)
    return x * 16 + y * 4 + z


def spread_materials(mats, rows, place):
    row = lax.broadcasted_iota(jnp.int32, (rows, rows), 0)
    col = lax.broadcasted_iota(jnp.int32, (rows, rows), 1)
    kept = jnp.where(place(row) == col, jnp.broadcast_to(mats.astype(f32), (rows, rows)), 0.0)
    return jnp.broadcast_to(jnp.sum(kept, axis=1, keepdims=True), (rows, 128))


def invert(blocks):
    row_id = lax.broadcasted_iota(jnp.int32, blocks.shape, 1)
    lane_id = lax.broadcasted_iota(jnp.int32, blocks.shape, 2)
    for k in range(MODES):
        pivot = 1.0 / blocks[:, k:k + 1, k:k + 1]
        at_lane = lane_id == k
        row = jnp.where(at_lane[:, :1, :], 1.0, blocks[:, k:k + 1, :]) * pivot
        column = blocks[:, :, k:k + 1]
        rest = jnp.where(at_lane, 0.0, blocks) - column * row
        blocks = jnp.where(row_id == k, row, rest)
    return blocks


def prepare(diag_ref, face_ref, prolong_ref, sweep_w, rest_w, inv_w, restrict_w, prolong_w):
    inverse = invert(diag_ref[...])

    def side(parts):
        return jnp.concatenate(parts, axis=1)

    def store(ref, at, w):
        high, low = pair(w)
        half = ref.shape[0] // 2
        ref[at:at + 128] = jnp.concatenate([high, high], axis=0)
        ref[half + at:half + at + 128] = jnp.concatenate([low, low], axis=0)
    store(inv_w, 0, WEIGHT * side([inverse[m] for m in range(MATERIALS)]))
    store(rest_w, 6 * 128, side([diag_ref[m] for m in range(MATERIALS)]))
    for d in range(6):
        turned = [jnp.transpose(face_ref[d, m]) for m in range(MATERIALS)]
        store(rest_w, d * 128, side(turned))
        mixed = [
            jnp.dot(turned[m], inverse[m], precision=highest, preferred_element_type=f32)
            for m in range(MATERIALS)
        ]
        store(sweep_w, d * 128, -WEIGHT * side(mixed))
    for c in range(8):
        block = SCALE * prolong_ref[c]
        store(restrict_w, c * 128, side([block, block]))
        back = jnp.transpose(prolong_ref[c])
        high, low = pair(side([back, back]))
        columns = slice(c * 128, c * 128 + 128)
        prolong_w[0:128, columns] = jnp.concatenate([high, high], axis=0)
        prolong_w[128:256, columns] = jnp.concatenate([low, low], axis=0)


def index_at(level, dim, *bits):
    at = [slice(None)] * len(TILE_DIMS[level])
    for i, b in enumerate(bits):
        at[3 * i + dim] = b
    return tuple(at)


def depth(level):
    return 2 - level


def face_tiles(value, level, dim, upper):
    tiles = value.reshape(TILE_DIMS[level] + (8, 128))
    return tiles[index_at(level, dim, *([1 if upper else 0] * depth(level)))].reshape(-1, 8, 128)


def pack_face(value, level, dim, upper):
    tiles = face_tiles(value, level, dim, upper)
    target = 0 if upper else 1
    amount = SUB[dim] if upper else -SUB[dim]
    count = tiles.shape[0]
    if count == 1:
        return roll_sub(tiles, amount).reshape(8, 128)
    half = count // 2
    packed = jnp.where(bit_is(dim, target), roll_sub(tiles[:half], amount), tiles[half:])
    half = half // 2
    packed = jnp.where(lanes(8) < 64, packed[:half], packed[half:])
    return packed.reshape(-1, 128)


def unpack_face(packed, level, dim, from_upper):
    amount = -SUB[dim] if from_upper else SUB[dim]
    if level == 2:
        return split(packed).reshape(1, 8, 128)
    other = swap_halves(packed)
    low_lanes = lanes(packed.shape[0]) < 64
    both = jnp.concatenate([jnp.where(low_lanes, packed, other), jnp.where(low_lanes, other, packed)], axis=0)
    both = split(both).reshape(-1, 8, 128)
    return jnp.concatenate([both, roll_sub(both, amount)], axis=0)


def border(tiles, halo, dim, up):
    rolled = roll_sub(tiles, SUB[dim] if up else -SUB[dim])
    return jnp.where(bit_is(dim, 0 if up else 1), rolled, halo.reshape(tiles.shape))


def place_inner(lhs, u, d):
    dim, up = d // 2, d % 2 == 0
    tiles = u.reshape(TILE_DIMS[0] + (8, 128))
    near, far = (0, 1) if up else (1, 0)

    def put(where, value):
        shape = value.shape[:-3] + (16, 128)
        lhs[(d,) + where] = value.reshape(shape).astype(bf16)
    put(index_at(0, dim, near)[:5], tiles[index_at(0, dim, far)])
    if dim < 2:
        put(index_at(0, dim, far, near)[:5], tiles[index_at(0, dim, near, far)])


def place_border(lhs, u, d, halo):
    dim, up = d // 2, d % 2 == 0
    tiles = u.reshape(TILE_DIMS[0] + (8, 128))
    near, far = (0, 1) if up else (1, 0)
    edge = border(tiles[index_at(0, dim, near, near)], halo, dim, up)
    if dim < 2:
        lhs[(d,) + index_at(0, dim, far, far)[:5]] = edge.reshape(edge.shape[:-3] + (16, 128)).astype(bf16)
    else:
        inner = tiles[index_at(0, dim, near, far)]
        both = [inner, edge] if up else [edge, inner]
        both = jnp.concatenate(both, axis=-2)
        lhs[d, :, :, far] = both.astype(bf16)


def shifted(u, level, d, halo):
    dim, up = d // 2, d % 2 == 0
    if level == 2:
        return border(u.reshape(1, 8, 128), halo, dim, up).reshape(8, 128)
    tiles = u.reshape(TILE_DIMS[1] + (8, 128))
    first = tiles[index_at(1, dim, 1 if up else 0)]
    edge = border(tiles[index_at(1, dim, 0 if up else 1)], halo, dim, up)
    parts = [first, edge] if up else [edge, first]
    return jnp.stack(parts, axis=dim).reshape(64, 128)


def kernel(
    sizes, rhs_ref, diag_ref, face_ref, prolong_ref, fine_ref, mid_ref, coarse_ref, out_ref,
    sweep_w, rest_w, inv_w, restrict_w, prolong_w, order, lhs,
    v0, f0, g0, m0, v1, f1, g1, m1, v2, g2, m2, out_box, in_box, send_sem, recv_sem,
):
    place = [lax.axis_index(axis) for axis in AXES]
    sides = []
    for d in range(6):
        dim, up = d // 2, d % 2 == 0
        there = list(place)
        there[dim] = place[dim] + (1 if up else -1)
        exists = (place[dim] < sizes[dim] - 1) if up else (place[dim] > 0)
        sides.append((exists, tuple(there)))

    barrier = pltpu.get_barrier_semaphore()
    for exists, there in sides:
        @pl.when(exists)
        def _():
            pl.semaphore_signal(barrier, inc=1, device_id=there, device_id_type=pl.DeviceIdType.MESH)
    pl.semaphore_wait(barrier, sum(exists.astype(jnp.int32) for exists, there in sides))
    for d, (exists, there) in enumerate(sides):
        @pl.when(jnp.logical_not(exists))
        def _():
            in_box[:, d] = jnp.zeros((2, 32, 128), f32)

    prepare(diag_ref, face_ref, prolong_ref, sweep_w, rest_w, inv_w, restrict_w, prolong_w)
    row = lax.broadcasted_iota(jnp.int32, (512, 512), 0)
    col = lax.broadcasted_iota(jnp.int32, (512, 512), 1)
    order[...] = jnp.where(element_of_row(row) == col, 1.0, 0.0).astype(bf16)
    m0[...] = lax.dot_general(
        order[...], jnp.broadcast_to(fine_ref[...].astype(f32), (128, 512)).astype(bf16),
        (((1,), (1,)), ((), ())), preferred_element_type=f32)
    m1[...] = spread_materials(mid_ref[...], 64, middle_of_row)
    m2[...] = spread_materials(coarse_ref[...], 8, lambda r: r)
    source = jnp.concatenate([rhs_ref[...], rhs_ref[...]], axis=0)
    total = None
    for piece in three(source):
        part = lax.dot_general(order[...], piece, (((1,), (1,)), ((), ())), preferred_element_type=f32)
        total = part if total is None else total + part
    f0[...] = total

    def scaled_inverse(value, material):
        return chosen(twice(split(value).astype(bf16), inv_w), material)

    g0[...] = scaled_inverse(f0[...], m0[...])
    v0[...] = g0[...]
    state = ((v0, g0, m0), (v1, g1, m1), (v2, g2, m2))

    def copy_of(d, level, slot):
        rows = pl.ds(0, FACE_ROWS[level])
        return pltpu.make_async_remote_copy(
            src_ref=out_box.at[slot, d, rows],
            dst_ref=in_box.at[slot, d ^ 1, rows],
            send_sem=send_sem.at[slot, d],
            recv_sem=recv_sem.at[slot, d ^ 1],
            device_id=sides[d][1],
            device_id_type=pl.DeviceIdType.MESH,
        )

    def arrival_of(d, level, slot):
        rows = pl.ds(0, FACE_ROWS[level])
        return pltpu.make_async_remote_copy(
            src_ref=out_box.at[slot, d, rows],
            dst_ref=in_box.at[slot, d, rows],
            send_sem=send_sem.at[slot, d],
            recv_sem=recv_sem.at[slot, d],
            device_id=sides[d][1],
            device_id_type=pl.DeviceIdType.MESH,
        )

    def gathered(level, step):
        slot = lax.rem(step, 2)
        value = state[level][0][...]
        for d in (4, 5, 2, 3, 0, 1):
            out_box[slot, d, :FACE_ROWS[level]] = pack_face(value, level, d // 2, d % 2 == 0)
        for d in (4, 5, 2, 3, 0, 1):
            @pl.when(sides[d][0])
            def _():
                copy_of(d, level, slot).start()
        u = split(value)
        if level == 0:
            for d in range(6):
                place_inner(lhs, u, d)
            lhs[6] = u.reshape(2, 2, 2, 2, 2, 16, 128).astype(bf16)
        for d in range(6):
            @pl.when(sides[d][0])
            def _():
                arrival_of(d, level, slot).wait_recv()
        fields = []
        for d in range(6):
            halo = unpack_face(in_box[slot, d, :FACE_ROWS[level]], level, d // 2, d % 2 == 0)
            if level == 0:
                place_border(lhs, u, d, halo)
            else:
                fields.append(shifted(u, level, d, halo))
        for d in range(6):
            @pl.when(sides[d][0])
            def _():
                copy_of(d, level, slot).wait_send()
        if level == 0:
            return [lhs[d].reshape(512, 128) for d in range(7)]
        fields.append(u)
        if level == 2:
            fields = [jnp.concatenate([field, field], axis=0) for field in fields]
        return [field.astype(bf16) for field in fields]

    def sweep(level, step):
        v, g, m = state[level]
        product = twice(jnp.concatenate(gathered(level, step)[:6], axis=1), sweep_w)
        v[...] = (1.0 - WEIGHT) * v[...] + g[...] + chosen(product[:ROWS[level]], m[...])

    def residual(level, step):
        f = (f0, f1)[level]
        product = twice(jnp.concatenate(gathered(level, step), axis=1), rest_w)
        return f[...] - chosen(product, state[level][2][...])

    def coarser(value):
        u = split(value)
        count = u.shape[0] // 8
        parts = [u[c * count:(c + 1) * count] for c in range(8)]
        if count == 8:
            parts = [jnp.concatenate([part, part], axis=0) for part in parts]
        return twice(jnp.concatenate(parts, axis=1).astype(bf16), restrict_w)[:count]

    def finer(value):
        u = split(value)
        count = u.shape[0]
        if count == 8:
            u = jnp.concatenate([u, u], axis=0)
        product = twice(u.astype(bf16), prolong_w)[:count]
        return jnp.concatenate([product[:, c * 128:(c + 1) * 128] for c in range(8)], axis=0)

    def wide(value):
        return jnp.concatenate([value, value], axis=0)

    @pl.loop(0, CYCLES)
    def _(cycle):
        base = 11 * cycle

        @pl.loop(0, SWEEPS - 1 + cycle)
        def _(i):
            sweep(0, base + i)
        f1[...] = coarser(residual(0, base + SWEEPS - 1 + cycle))
        base = base + SWEEPS + cycle
        g1[...] = scaled_inverse(f1[...], m1[...])
        v1[...] = g1[...]
        for i in range(SWEEPS - 1):
            sweep(1, base + i)
        base = base + SWEEPS - 1
        f2 = coarser(residual(1, base))
        base = base + 1
        g2[...] = scaled_inverse(wide(f2), wide(m2[...]))[:8]
        v2[...] = g2[...]

        @pl.loop(0, COARSE_SWEEPS - 1)
        def _(i):
            sweep(2, base + i)
        base = base + COARSE_SWEEPS - 1
        v1[...] = v1[...] + finer(v2[...])

        @pl.loop(0, SWEEPS)
        def _(i):
            sweep(1, base + i)
        base = base + SWEEPS
        v0[...] = v0[...] + finer(v1[...])

        @pl.loop(0, SWEEPS)
        def _(i):
            sweep(0, base + i)

    result = jnp.transpose(v0[...])[:MODES]
    total = None
    for piece in three(result):
        part = jnp.dot(piece, order[...], preferred_element_type=f32)
        total = part if total is None else total + part
    out_ref[...] = total


def per_device(sizes, right_side, diag_blocks, face_blocks, prolong, mats_fine, mats_mid, mats_coarse):
    def vmem(shape, dtype=f32):
        return pltpu.VMEM(shape, dtype)
    field = [vmem((512, 128))] * 4
    middle = [vmem((64, 128))] * 4
    coarse = [vmem((8, 128))] * 3
    result = pl.pallas_call(
        partial(kernel, sizes),
        out_shape=jax.ShapeDtypeStruct((MODES, 512), f32),
        in_specs=[pl.BlockSpec(memory_space=pltpu.VMEM)] * 7,
        out_specs=pl.BlockSpec(memory_space=pltpu.VMEM),
        scratch_shapes=[
            vmem((2 * 768, 256), bf16),
            vmem((2 * 896, 256), bf16),
            vmem((2 * 128, 256), bf16),
            vmem((2 * 1024, 128), bf16),
            vmem((2 * 128, 1024), bf16),
            vmem((512, 512), bf16),
            vmem((7, 2, 2, 2, 2, 2, 16, 128), bf16),
        ] + field + middle + coarse + [
            vmem((2, 6, 32, 128)),
            vmem((2, 6, 32, 128)),
            pltpu.SemaphoreType.DMA((2, 6)),
            pltpu.SemaphoreType.DMA((2, 6)),
        ],
        compiler_params=pltpu.CompilerParams(collective_id=0, has_side_effects=True),
        name="cycles",
    )(
        right_side[0, 0, 0], diag_blocks, face_blocks, prolong,
        mats_fine.reshape(1, -1), mats_mid.reshape(1, -1), mats_coarse.reshape(1, -1),
    )
    return result[None, None, None]


def solution(mesh):
    placed = (
        P("gx", "gy", "gz", None, None),
        P(),
        P(),
        P(),
        P("gx", "gy", "gz", None),
        P("gx", "gy", "gz", None),
        P("gx", "gy", "gz", None),
    )
    sizes = tuple(mesh.shape[axis] for axis in AXES)
    return jax.shard_map(
        partial(per_device, sizes),
        mesh=mesh,
        in_specs=placed,
        out_specs=P("gx", "gy", "gz", None, None),
        check_vma=False,
    )
```

time: 830 us -> 148 us (0.18)
  the two profiles are of different devices: /device:TPU:97 before, /device:TPU:28 now
where the time goes in v1:
time: 148 us
  Pallas kernels  147 us (99%)
  local copies, waits for them, and re-layouts  1.57 us (1%)
    pallas_call x1, Pallas kernels, per_device(): pl.pallas_call(partial(kernel, sizes), out_shape=jax.ShapeDtypeStruct((MO...  147 us

profile of v1, /device:TPU:28, one launch (start us, length us, event | category | flops | bytes accessed | tf_op | source)
XLA Modules:
  0.0 148.3 jit_solution(8458326755604853646)
XLA Ops:
  0.0 146.7 %cycles.1 = f32[64,512]{1,0:T(8,128)} custom-call(f32[64,512]{1,0:T(8,128)} %bitcast.6, f32[4,64,64]{2,1,0:T(8,128)} %diag_ref.1, f32[6,4,64,64]{3,2,1,0:T(8,128)} %face_ref.1, f32[8,64,64]{2,1,0:T(8,128)} %prolong_ref.1, s32[1,512]{1,0:T(1,128)} %bitcast.7, s32[1,64]{1,0:T(1,128)} %bitcast.8, s32[1,8]{1,0:T(1,128)} %bitcast.9), custom_call_target="tpu_custom_call" | custom-call | tf_op jit(solution)/shard_map/cycles/pallas_call | solution.py:411
  146.7 1.6 %copy.9 = f32[1,1,1,64,512]{4,3,2,1,0:T(8,128)} copy(f32[1,1,1,64,512]{4,3,2,1,0:T(8,128)} %bitcast.5) | data formatting | bytes 262144

commit v2 on v1

--- a/solution.py
+++ b/solution.py
@@ -151,34 +151,74 @@
     return 2 - level
 
 
-def face_tiles(value, level, dim, upper):
-    tiles = value.reshape(TILE_DIMS[level] + (8, 128))
-    return tiles[index_at(level, dim, *([1 if upper else 0] * depth(level)))].reshape(-1, 8, 128)
-
-
-def pack_face(value, level, dim, upper):
-    tiles = face_tiles(value, level, dim, upper)
-    target = 0 if upper else 1
-    amount = SUB[dim] if upper else -SUB[dim]
-    count = tiles.shape[0]
-    if count == 1:
-        return roll_sub(tiles, amount).reshape(8, 128)
-    half = count // 2
-    packed = jnp.where(bit_is(dim, target), roll_sub(tiles[:half], amount), tiles[half:])
+PAIRS = ((0, 1), (0, 2), (1, 2))
+EDGES = tuple((p, q, sp, sq) for p, q in PAIRS for sp in (0, 1) for sq in (0, 1))
+SLOTS = 3
+
+
+def own_tiles(value, level):
+    return value.reshape(TILE_DIMS[level] + (8, 128))
+
+
+def outer(tiles, level, dim, upper, layer):
+    bits = [upper] * depth(level)
+    if layer == 2 and bits:
+        bits[0] = 1 - upper
+    return tiles[index_at(level, dim, *bits)].reshape(-1, 8, 128)
+
+
+def toward(dim, upper):
+    return SUB[dim] if upper else -SUB[dim]
+
+
+def two_halves(packed):
+    other = swap_halves(packed.reshape(-1, 128)).reshape(packed.shape)
+    low_lanes = lanes(8) < 64
+    return jnp.concatenate([jnp.where(low_lanes, packed, other), jnp.where(low_lanes, other, packed)], axis=0)
+
+
+def pack_face(tiles, level, dim, upper, layer):
+    tiles = outer(tiles, level, dim, upper, layer)
+    half = tiles.shape[0] // 2
+    packed = jnp.where(bit_is(dim, 1 - upper), roll_sub(tiles[:half], toward(dim, upper)), tiles[half:])
     half = half // 2
-    packed = jnp.where(lanes(8) < 64, packed[:half], packed[half:])
-    return packed.reshape(-1, 128)
-
-
-def unpack_face(packed, level, dim, from_upper):
-    amount = -SUB[dim] if from_upper else SUB[dim]
+    return jnp.where(lanes(8) < 64, packed[:half], packed[half:]).reshape(-1, 128)
+
+
+def unpack_face(packed, level, dim, upper, layer):
+    packed = packed.reshape(-1, 8, 128)
     if level == 2:
-        return split(packed).reshape(1, 8, 128)
-    other = swap_halves(packed)
-    low_lanes = lanes(packed.shape[0]) < 64
-    both = jnp.concatenate([jnp.where(low_lanes, packed, other), jnp.where(low_lanes, other, packed)], axis=0)
-    both = split(both).reshape(-1, 8, 128)
-    return jnp.concatenate([both, roll_sub(both, amount)], axis=0)
+        return packed if layer == 2 else roll_sub(packed, -toward(dim, upper))
+    both = two_halves(packed)
+    return jnp.concatenate([both, roll_sub(both, -toward(dim, upper))], axis=0)
+
+
+def pack_edge(tiles, level, p, q, sp, sq):
+    at = list(index_at(level, p, *([sp] * depth(level))))
+    for i, b in enumerate(index_at(level, q, *([sq] * depth(level)))):
+        at[i] = b if at[i] == slice(None) else at[i]
+    tiles = tiles[tuple(at)].reshape(-1, 8, 128)
+    half = tiles.shape[0] // 2
+    if level == 0:
+        moved = roll_sub(tiles[:half], toward(p, sp) + toward(q, sq))
+        tiles = jnp.where(bit_is(p, 1 - sp), moved, roll_sub(tiles[half:], toward(q, sq)))
+    else:
+        tiles = roll_sub(tiles, toward(p, sp) + toward(q, sq))
+    return jnp.where(lanes(8) < 64, tiles[0], tiles[1])
+
+
+def unpack_edge(packed, level, p, q, sp, sq):
+    packed = packed.reshape(1, 8, 128)
+    if level == 2:
+        return roll_sub(packed, -toward(p, sp) - toward(q, sq))
+    both = two_halves(packed)
+    if level == 1:
+        return both
+    return jnp.concatenate([both, roll_sub(both, -toward(p, sp))], axis=0)
+
+
+def split_tiles(tiles):
+    return split(tiles.reshape(-1, 128)).reshape(tiles.shape)
 
 
 def border(tiles, halo, dim, up):
@@ -186,9 +226,30 @@
     return jnp.where(bit_is(dim, 0 if up else 1), rolled, halo.reshape(tiles.shape))
 
 
+def take(tiles, axis, bit):
+    at = [slice(None)] * tiles.ndim
+    at[axis] = bit
+    return tiles[tuple(at)]
+
+
+def shifted(tiles, axes, dim, up, halo):
+    if not axes:
+        return border(tiles, halo, dim, up)
+    near, far = (0, 1) if up else (1, 0)
+
+    def ordered(at_near, at_far, axis):
+        return jnp.stack([at_near, at_far] if up else [at_far, at_near], axis=axis)
+    if len(axes) == 1:
+        return ordered(take(tiles, axes[0], far), border(take(tiles, axes[0], near), halo, dim, up), axes[0])
+    kept = take(tiles, axes[0], near)
+    deeper = axes[1] - 1
+    end = border(take(kept, deeper, near), halo, dim, up)
+    return ordered(take(tiles, axes[0], far), ordered(take(kept, deeper, far), end, deeper), axes[0])
+
+
 def place_inner(lhs, u, d):
     dim, up = d // 2, d % 2 == 0
-    tiles = u.reshape(TILE_DIMS[0] + (8, 128))
+    tiles = own_tiles(u, 0)
     near, far = (0, 1) if up else (1, 0)
 
     def put(where, value):
@@ -201,7 +262,7 @@
 
 def place_border(lhs, u, d, halo):
     dim, up = d // 2, d % 2 == 0
-    tiles = u.reshape(TILE_DIMS[0] + (8, 128))
+    tiles = own_tiles(u, 0)
     near, far = (0, 1) if up else (1, 0)
     edge = border(tiles[index_at(0, dim, near, near)], halo, dim, up)
     if dim < 2:
@@ -213,43 +274,81 @@
         lhs[d, :, :, far] = both.astype(bf16)
 
 
-def shifted(u, level, d, halo):
-    dim, up = d // 2, d % 2 == 0
-    if level == 2:
-        return border(u.reshape(1, 8, 128), halo, dim, up).reshape(8, 128)
-    tiles = u.reshape(TILE_DIMS[1] + (8, 128))
-    first = tiles[index_at(1, dim, 1 if up else 0)]
-    edge = border(tiles[index_at(1, dim, 0 if up else 1)], halo, dim, up)
-    parts = [first, edge] if up else [edge, first]
-    return jnp.stack(parts, axis=dim).reshape(64, 128)
+def halo_fields(u, level, dim, near, far, edges):
+    tiles = own_tiles(u, level)
+    others = [i for i in range(3) if i != dim]
+    bits = near.reshape((2,) * (2 * depth(level)) + (8, 128))
+    fields = []
+    for d in range(6):
+        along, up = d // 2, d % 2 == 0
+        if along == dim:
+            own = outer(tiles, level, dim, 0 if up else 1, 1)
+            field = jnp.where(bit_is(dim, 1 if up else 0), far, own)
+        else:
+            axes = [others.index(along) + 2 * i for i in range(depth(level))]
+            field = shifted(bits, axes, along, up, edges[PAIRS.index((min(dim, along), max(dim, along)))])
+        fields.append(field.reshape(-1, 128))
+    return jnp.concatenate(fields, axis=1)
 
 
 def kernel(
     sizes, rhs_ref, diag_ref, face_ref, prolong_ref, fine_ref, mid_ref, coarse_ref, out_ref,
     sweep_w, rest_w, inv_w, restrict_w, prolong_w, order, lhs,
-    v0, f0, g0, m0, v1, f1, g1, m1, v2, g2, m2, out_box, in_box, send_sem, recv_sem,
+    v0, f0, g0, m0, v1, f1, g1, m1, v2, g2, m2,
+    halo_g0, halo_g1, halo_g2, halo_m0, halo_m1, halo_m2,
+    out_face, in_face, out_edge, in_edge, out_mat, in_mat,
+    send_face, recv_face, send_edge, recv_edge, send_mat, recv_mat,
 ):
     place = [lax.axis_index(axis) for axis in AXES]
-    sides = []
-    for d in range(6):
-        dim, up = d // 2, d % 2 == 0
+    able = [((place[i] > 0), (place[i] < sizes[i] - 1)) for i in range(3)]
+
+    def device(*moves):
         there = list(place)
-        there[dim] = place[dim] + (1 if up else -1)
-        exists = (place[dim] < sizes[dim] - 1) if up else (place[dim] > 0)
-        sides.append((exists, tuple(there)))
+        for dim, upper in moves:
+            there[dim] = there[dim] + (1 if upper else -1)
+        return tuple(there)
+    sides = [(able[dim][upper], device((dim, upper))) for dim in range(3) for upper in (1, 0)]
+    corners = [(able[p][sp] & able[q][sq], device((p, sp), (q, sq))) for p, q, sp, sq in EDGES]
+    first = (4, 5, 2, 3, 0, 1)
+    first_edges = (4, 5, 6, 7, 8, 9, 10, 11, 0, 1, 2, 3)
 
     barrier = pltpu.get_barrier_semaphore()
-    for exists, there in sides:
+    for exists, there in sides + corners:
         @pl.when(exists)
         def _():
             pl.semaphore_signal(barrier, inc=1, device_id=there, device_id_type=pl.DeviceIdType.MESH)
-    pl.semaphore_wait(barrier, sum(exists.astype(jnp.int32) for exists, there in sides))
+    pl.semaphore_wait(barrier, sum(exists.astype(jnp.int32) for exists, there in sides + corners))
     for d, (exists, there) in enumerate(sides):
         @pl.when(jnp.logical_not(exists))
         def _():
-            in_box[:, d] = jnp.zeros((2, 32, 128), f32)
-
-    prepare(diag_ref, face_ref, prolong_ref, sweep_w, rest_w, inv_w, restrict_w, prolong_w)
+            in_face[:, d] = jnp.zeros((SLOTS, 64, 128), f32)
+            in_mat[:, d] = jnp.zeros((3, 32, 128), f32)
+    for e, (exists, there) in enumerate(corners):
+        @pl.when(jnp.logical_not(exists))
+        def _():
+            in_edge[:, e] = jnp.zeros((SLOTS, 8, 128), f32)
+
+    def remote(src, dst, send, recv, there):
+        return pltpu.make_async_remote_copy(
+            src_ref=src, dst_ref=dst, send_sem=send, recv_sem=recv,
+            device_id=there, device_id_type=pl.DeviceIdType.MESH)
+
+    def face_copy(d, land, slot, rows, raw):
+        rows = pl.ds(0, rows)
+        return remote(
+            out_face.at[slot, 0 if raw else d, rows], in_face.at[slot, land, rows],
+            send_face.at[slot, d], recv_face.at[slot, land], sides[d][1])
+
+    def edge_copy(e, land, slot, raw):
+        src = out_face.at[slot, 0, pl.ds(0, 8)] if raw else out_edge.at[slot, e]
+        return remote(src, in_edge.at[slot, land], send_edge.at[slot, e], recv_edge.at[slot, land], corners[e][1])
+
+    def mat_copy(d, land, level):
+        rows = pl.ds(0, FACE_ROWS[level])
+        return remote(
+            out_mat.at[level, d, rows], in_mat.at[level, land, rows],
+            send_mat.at[level, d], recv_mat.at[level, land], sides[d][1])
+
     row = lax.broadcasted_iota(jnp.int32, (512, 512), 0)
     col = lax.broadcasted_iota(jnp.int32, (512, 512), 1)
     order[...] = jnp.where(element_of_row(row) == col, 1.0, 0.0).astype(bf16)
@@ -258,6 +357,18 @@
         (((1,), (1,)), ((), ())), preferred_element_type=f32)
     m1[...] = spread_materials(mid_ref[...], 64, middle_of_row)
     m2[...] = spread_materials(coarse_ref[...], 8, lambda r: r)
+    for level, m in enumerate((m0, m1, m2)):
+        tiles = own_tiles(m[...] + 1.0, level)
+        for d in first:
+            packed = tiles if level == 2 else pack_face(tiles, level, d // 2, 1 - d % 2, 1)
+            out_mat[level, d, :FACE_ROWS[level]] = packed
+    for level in range(3):
+        for d in first:
+            @pl.when(sides[d][0])
+            def _():
+                mat_copy(d, d ^ 1, level).start()
+
+    prepare(diag_ref, face_ref, prolong_ref, sweep_w, rest_w, inv_w, restrict_w, prolong_w)
     source = jnp.concatenate([rhs_ref[...], rhs_ref[...]], axis=0)
     total = None
     for piece in three(source):
@@ -271,38 +382,43 @@
     g0[...] = scaled_inverse(f0[...], m0[...])
     v0[...] = g0[...]
     state = ((v0, g0, m0), (v1, g1, m1), (v2, g2, m2))
-
-    def copy_of(d, level, slot):
-        rows = pl.ds(0, FACE_ROWS[level])
-        return pltpu.make_async_remote_copy(
-            src_ref=out_box.at[slot, d, rows],
-            dst_ref=in_box.at[slot, d ^ 1, rows],
-            send_sem=send_sem.at[slot, d],
-            recv_sem=recv_sem.at[slot, d ^ 1],
-            device_id=sides[d][1],
-            device_id_type=pl.DeviceIdType.MESH,
-        )
-
-    def arrival_of(d, level, slot):
-        rows = pl.ds(0, FACE_ROWS[level])
-        return pltpu.make_async_remote_copy(
-            src_ref=out_box.at[slot, d, rows],
-            dst_ref=in_box.at[slot, d, rows],
-            send_sem=send_sem.at[slot, d],
-            recv_sem=recv_sem.at[slot, d],
-            device_id=sides[d][1],
-            device_id_type=pl.DeviceIdType.MESH,
-        )
-
-    def gathered(level, step):
-        slot = lax.rem(step, 2)
+    halos = ((halo_g0, halo_m0), (halo_g1, halo_m1), (halo_g2, halo_m2))
+
+    def merged(read, level, dim, layer):
+        above = unpack_face(read(2 * dim), level, dim, 1, layer)
+        below = unpack_face(read(2 * dim + 1), level, dim, 0, layer)
+        return jnp.where(bit_is(dim, 1), above, below)
+
+    def exchange(level, step, deep):
+        slot = lax.rem(step, SLOTS)
+        rows = FACE_ROWS[level]
+        raw = level == 2
+        layers = 2 if deep and not raw else 1
         value = state[level][0][...]
-        for d in (4, 5, 2, 3, 0, 1):
-            out_box[slot, d, :FACE_ROWS[level]] = pack_face(value, level, d // 2, d % 2 == 0)
-        for d in (4, 5, 2, 3, 0, 1):
-            @pl.when(sides[d][0])
-            def _():
-                copy_of(d, level, slot).start()
+        tiles = own_tiles(value, level)
+        if raw:
+            out_face[slot, 0, :8] = value
+        else:
+            for d in first:
+                for layer in range(layers):
+                    out_face[slot, d, layer * rows:layer * rows + rows] = pack_face(
+                        tiles, level, d // 2, 1 - d % 2, layer + 1)
+                @pl.when(sides[d][0])
+                def _():
+                    face_copy(d, d ^ 1, slot, layers * rows, raw).start()
+            if deep:
+                for e in first_edges:
+                    out_edge[slot, e] = pack_edge(tiles, level, *EDGES[e])
+        if raw:
+            for d in first:
+                @pl.when(sides[d][0])
+                def _():
+                    face_copy(d, d ^ 1, slot, layers * rows, raw).start()
+        if deep:
+            for e in first_edges:
+                @pl.when(corners[e][0])
+                def _():
+                    edge_copy(e, e ^ 3, slot, raw).start()
         u = split(value)
         if level == 0:
             for d in range(6):
@@ -311,34 +427,103 @@
         for d in range(6):
             @pl.when(sides[d][0])
             def _():
-                arrival_of(d, level, slot).wait_recv()
-        fields = []
-        for d in range(6):
-            halo = unpack_face(in_box[slot, d, :FACE_ROWS[level]], level, d // 2, d % 2 == 0)
-            if level == 0:
-                place_border(lhs, u, d, halo)
-            else:
-                fields.append(shifted(u, level, d, halo))
+                face_copy(d, d, slot, layers * rows, raw).wait_recv()
+        if deep:
+            for e in range(12):
+                @pl.when(corners[e][0])
+                def _():
+                    edge_copy(e, e, slot, raw).wait_recv()
+        near = [merged(lambda d: in_face[slot, d, :rows], level, dim, 1) for dim in range(3)]
+        far, edges = None, None
+        if deep:
+            at = 0 if raw else rows
+            far = [
+                split_tiles(merged(lambda d: in_face[slot, d, at:at + rows], level, dim, 2)) for dim in range(3)
+            ]
+            edges = []
+            for p, q in PAIRS:
+                got = [
+                    unpack_edge(in_edge[slot, e], level, p, q, sp, sq)
+                    for e, (p_, q_, sp, sq) in enumerate(EDGES) if (p_, q_) == (p, q)
+                ]
+                got = [jnp.where(bit_is(q, 1), got[1], got[0]), jnp.where(bit_is(q, 1), got[3], got[2])]
+                edges.append(split_tiles(jnp.where(bit_is(p, 1), got[1], got[0])))
         for d in range(6):
             @pl.when(sides[d][0])
             def _():
-                copy_of(d, level, slot).wait_send()
+                face_copy(d, d ^ 1, slot, layers * rows, raw).wait_send()
+        if deep:
+            for e in range(12):
+                @pl.when(corners[e][0])
+                def _():
+                    edge_copy(e, e ^ 3, slot, raw).wait_send()
+        return u, near, far, edges
+
+    def gathered(level, u, planes):
         if level == 0:
+            for d in range(6):
+                place_border(lhs, u, d, planes[d // 2])
             return [lhs[d].reshape(512, 128) for d in range(7)]
+        fields = []
+        for d in range(6):
+            dim = d // 2
+            field = shifted(own_tiles(u, level), (dim,) if level == 1 else (), dim, d % 2 == 0, planes[dim])
+            fields.append(field.reshape(-1, 128))
         fields.append(u)
         if level == 2:
             fields = [jnp.concatenate([field, field], axis=0) for field in fields]
         return [field.astype(bf16) for field in fields]
 
-    def sweep(level, step):
+    def relaxed(level, value, u, planes):
         v, g, m = state[level]
-        product = twice(jnp.concatenate(gathered(level, step)[:6], axis=1), sweep_w)
-        v[...] = (1.0 - WEIGHT) * v[...] + g[...] + chosen(product[:ROWS[level]], m[...])
-
-    def residual(level, step):
+        product = twice(jnp.concatenate(gathered(level, u, planes)[:6], axis=1), sweep_w)
+        return (1.0 - WEIGHT) * value + g[...] + chosen(product[:ROWS[level]], m[...])
+
+    def residual(level, u, planes):
         f = (f0, f1)[level]
-        product = twice(jnp.concatenate(gathered(level, step), axis=1), rest_w)
+        product = twice(jnp.concatenate(gathered(level, u, planes), axis=1), rest_w)
         return f[...] - chosen(product, state[level][2][...])
+
+    def refilled(u):
+        for d in range(6):
+            place_inner(lhs, u, d)
+        lhs[6] = u.reshape(2, 2, 2, 2, 2, 16, 128).astype(bf16)
+
+    def double_step(level, step, fresh, last):
+        v = state[level][0]
+        halo_g, halo_m = halos[level]
+        u, near, far, edges = exchange(level, step, True)
+        planes = [split_tiles(tiles) for tiles in near]
+        raw = jnp.concatenate([tiles.reshape(-1, 128) for tiles in near], axis=0)
+        if fresh:
+            halo_g[...] = raw
+        rows = [halo_fields(u, level, dim, planes[dim], far[dim], edges) for dim in range(3)]
+        rows = jnp.concatenate(rows, axis=0)
+        count = rows.shape[0]
+        if count % 16:
+            rows = jnp.concatenate([rows, rows[:16 - count % 16]], axis=0)
+        value = relaxed(level, v[...], u, planes)
+        product = twice(rows.astype(bf16), sweep_w)[:count]
+        raw = (1.0 - WEIGHT) * raw + halo_g[...] + chosen(product, halo_m[...])
+        planes = split(raw).reshape(3, -1, 8, 128)
+        planes = [planes[dim] for dim in range(3)]
+        u = split(value)
+        if level == 0:
+            refilled(u)
+        if last == "sweep":
+            v[...] = relaxed(level, value, u, planes)
+            return None
+        v[...] = value
+        return residual(level, u, planes)
+
+    def single_step(level, step, last):
+        v = state[level][0]
+        u, near, far, edges = exchange(level, step, False)
+        planes = [split_tiles(tiles) for tiles in near]
+        if last == "sweep":
+            v[...] = relaxed(level, v[...], u, planes)
+            return None
+        return residual(level, u, planes)
 
     def coarser(value):
         u = split(value)
@@ -359,40 +544,40 @@
     def wide(value):
         return jnp.concatenate([value, value], axis=0)
 
+    for level in range(3):
+        for d in range(6):
+            @pl.when(sides[d][0])
+            def _():
+                mat_copy(d, d, level).wait_recv()
+                mat_copy(d, d ^ 1, level).wait_send()
+        planes = [
+            merged(lambda d: in_mat[level, d, :FACE_ROWS[level]], level, dim, 1).reshape(-1, 128)
+            for dim in range(3)
+        ]
+        halos[level][1][...] = jnp.concatenate(planes, axis=0) - 1.0
+
     @pl.loop(0, CYCLES)
     def _(cycle):
-        base = 11 * cycle
-
-        @pl.loop(0, SWEEPS - 1 + cycle)
-        def _(i):
-            sweep(0, base + i)
-        f1[...] = coarser(residual(0, base + SWEEPS - 1 + cycle))
-        base = base + SWEEPS + cycle
+        @pl.when(cycle == 0)
+        def _():
+            f1[...] = coarser(double_step(0, 0, True, "residual"))
+
+        @pl.when(cycle > 0)
+        def _():
+            double_step(0, 6, False, "sweep")
+            f1[...] = coarser(single_step(0, 7, "residual"))
+        base = 1 + 7 * cycle
         g1[...] = scaled_inverse(f1[...], m1[...])
         v1[...] = g1[...]
-        for i in range(SWEEPS - 1):
-            sweep(1, base + i)
-        base = base + SWEEPS - 1
-        f2 = coarser(residual(1, base))
-        base = base + 1
+        f2 = coarser(double_step(1, base, True, "residual"))
         g2[...] = scaled_inverse(wide(f2), wide(m2[...]))[:8]
         v2[...] = g2[...]
-
-        @pl.loop(0, COARSE_SWEEPS - 1)
-        def _(i):
-            sweep(2, base + i)
-        base = base + COARSE_SWEEPS - 1
+        double_step(2, base + 1, True, "sweep")
+        single_step(2, base + 2, "sweep")
         v1[...] = v1[...] + finer(v2[...])
-
-        @pl.loop(0, SWEEPS)
-        def _(i):
-            sweep(1, base + i)
-        base = base + SWEEPS
+        double_step(1, base + 3, False, "sweep")
         v0[...] = v0[...] + finer(v1[...])
-
-        @pl.loop(0, SWEEPS)
-        def _(i):
-            sweep(0, base + i)
+        double_step(0, base + 4, False, "sweep")
 
     result = jnp.transpose(v0[...])[:MODES]
     total = None
@@ -421,11 +606,16 @@
             vmem((2 * 128, 1024), bf16),
             vmem((512, 512), bf16),
             vmem((7, 2, 2, 2, 2, 2, 16, 128), bf16),
-        ] + field + middle + coarse + [
-            vmem((2, 6, 32, 128)),
-            vmem((2, 6, 32, 128)),
-            pltpu.SemaphoreType.DMA((2, 6)),
-            pltpu.SemaphoreType.DMA((2, 6)),
+        ] + field + middle + coarse + [vmem((3 * n, 128)) for n in (128, 32, 8)] * 2 + [
+            vmem((SLOTS, 6, 64, 128)),
+            vmem((SLOTS, 6, 64, 128)),
+            vmem((SLOTS, 12, 8, 128)),
+            vmem((SLOTS, 12, 8, 128)),
+            vmem((3, 6, 32, 128)),
+            vmem((3, 6, 32, 128)),
+        ] + [pltpu.SemaphoreType.DMA((SLOTS, n)) for n in (6, 6, 12, 12)] + [
+            pltpu.SemaphoreType.DMA((3, 6)),
+            pltpu.SemaphoreType.DMA((3, 6)),
         ],
         compiler_params=pltpu.CompilerParams(collective_id=0, has_side_effects=True),
         name="cycles",

time: 148 us -> 141 us (0.953)
  the two profiles are of different devices: /device:TPU:28 before, /device:TPU:12 now
where the time goes in v2:
time: 141 us
  Pallas kernels  139 us (99%)
  local copies, waits for them, and re-layouts  1.57 us (1%)
    pallas_call x1, Pallas kernels, per_device(): pl.pallas_call(partial(kernel, sizes), out_shape=jax.ShapeDtypeStruct((MO...  139 us

profile of v2, /device:TPU:12, one launch (start us, length us, event | category | flops | bytes accessed | tf_op | source)
XLA Modules:
  0.0 140.6 jit_solution(14085871837742686989)
XLA Ops:
  0.0 139.0 %cycles.1 = f32[64,512]{1,0:T(8,128)} custom-call(f32[64,512]{1,0:T(8,128)} %bitcast.6, f32[4,64,64]{2,1,0:T(8,128)} %diag_ref.1, f32[6,4,64,64]{3,2,1,0:T(8,128)} %face_ref.1, f32[8,64,64]{2,1,0:T(8,128)} %prolong_ref.1, s32[1,512]{1,0:T(1,128)} %bitcast.7, s32[1,64]{1,0:T(1,128)} %bitcast.8, s32[1,8]{1,0:T(1,128)} %bitcast.9), custom_call_target="tpu_custom_call" | custom-call | tf_op jit(solution)/shard_map/cycles/pallas_call | solution.py:596
  139.0 1.6 %copy.9 = f32[1,1,1,64,512]{4,3,2,1,0:T(8,128)} copy(f32[1,1,1,64,512]{4,3,2,1,0:T(8,128)} %bitcast.5) | data formatting | bytes 262144

commit v3 on v2

--- a/solution.py
+++ b/solution.py
@@ -298,26 +298,51 @@
     halo_g0, halo_g1, halo_g2, halo_m0, halo_m1, halo_m2,
     out_face, in_face, out_edge, in_edge, out_mat, in_mat,
     send_face, recv_face, send_edge, recv_edge, send_mat, recv_mat,
+    rhs_box, fine_box, mid_box, coarse_box, result, send_block, recv_block,
 ):
-    place = [lax.axis_index(axis) for axis in AXES]
+    home = tuple(lax.axis_index(axis) for axis in AXES)
+    run = sizes[1] // sizes[2]
+    shift = run // 2
+
+    def holder(x, y, z):
+        along = lax.rem(y + shift + sizes[1], sizes[1])
+        return x, z * run + lax.rem(along, run), along // run
+    worker = holder(*home)
+    along = home[2] * run + lax.rem(home[1], run)
+    place = [home[0], lax.rem(along - shift + sizes[1], sizes[1]), home[1] // run]
+    owner = tuple(place)
     able = [((place[i] > 0), (place[i] < sizes[i] - 1)) for i in range(3)]
 
     def device(*moves):
         there = list(place)
         for dim, upper in moves:
             there[dim] = there[dim] + (1 if upper else -1)
-        return tuple(there)
+        return holder(*there)
     sides = [(able[dim][upper], device((dim, upper))) for dim in range(3) for upper in (1, 0)]
     corners = [(able[p][sp] & able[q][sq], device((p, sp), (q, sq))) for p, q, sp, sq in EDGES]
-    first = (4, 5, 2, 3, 0, 1)
-    first_edges = (4, 5, 6, 7, 8, 9, 10, 11, 0, 1, 2, 3)
+    first = (2, 3, 4, 5, 0, 1)
+    first_edges = (8, 9, 10, 11, 0, 1, 2, 3, 4, 5, 6, 7)
 
     barrier = pltpu.get_barrier_semaphore()
     for exists, there in sides + corners:
         @pl.when(exists)
         def _():
             pl.semaphore_signal(barrier, inc=1, device_id=there, device_id_type=pl.DeviceIdType.MESH)
-    pl.semaphore_wait(barrier, sum(exists.astype(jnp.int32) for exists, there in sides + corners))
+    for there in (worker, owner):
+        pl.semaphore_signal(barrier, inc=1, device_id=there, device_id_type=pl.DeviceIdType.MESH)
+    pl.semaphore_wait(barrier, 2 + sum(exists.astype(jnp.int32) for exists, there in sides + corners))
+
+    def remote(src, dst, send, recv, there):
+        return pltpu.make_async_remote_copy(
+            src_ref=src, dst_ref=dst, send_sem=send, recv_sem=recv,
+            device_id=there, device_id_type=pl.DeviceIdType.MESH)
+    moved = [
+        remote(src, dst, send_block.at[i], recv_block.at[i], worker)
+        for i, (src, dst) in enumerate((
+            (fine_ref, fine_box), (mid_ref, mid_box), (coarse_ref, coarse_box), (rhs_ref, rhs_box)))
+    ]
+    for copy in moved:
+        copy.start()
     for d, (exists, there) in enumerate(sides):
         @pl.when(jnp.logical_not(exists))
         def _():
@@ -328,11 +353,6 @@
         def _():
             in_edge[:, e] = jnp.zeros((SLOTS, 8, 128), f32)
 
-    def remote(src, dst, send, recv, there):
-        return pltpu.make_async_remote_copy(
-            src_ref=src, dst_ref=dst, send_sem=send, recv_sem=recv,
-            device_id=there, device_id_type=pl.DeviceIdType.MESH)
-
     def face_copy(d, land, slot, rows, raw):
         rows = pl.ds(0, rows)
         return remote(
@@ -352,11 +372,14 @@
     row = lax.broadcasted_iota(jnp.int32, (512, 512), 0)
     col = lax.broadcasted_iota(jnp.int32, (512, 512), 1)
     order[...] = jnp.where(element_of_row(row) == col, 1.0, 0.0).astype(bf16)
+    prepare(diag_ref, face_ref, prolong_ref, sweep_w, rest_w, inv_w, restrict_w, prolong_w)
+    for copy in moved[:3]:
+        copy.wait()
     m0[...] = lax.dot_general(
-        order[...], jnp.broadcast_to(fine_ref[...].astype(f32), (128, 512)).astype(bf16),
+        order[...], jnp.broadcast_to(fine_box[...].astype(f32), (128, 512)).astype(bf16),
         (((1,), (1,)), ((), ())), preferred_element_type=f32)
-    m1[...] = spread_materials(mid_ref[...], 64, middle_of_row)
-    m2[...] = spread_materials(coarse_ref[...], 8, lambda r: r)
+    m1[...] = spread_materials(mid_box[...], 64, middle_of_row)
+    m2[...] = spread_materials(coarse_box[...], 8, lambda r: r)
     for level, m in enumerate((m0, m1, m2)):
         tiles = own_tiles(m[...] + 1.0, level)
         for d in first:
@@ -368,8 +391,8 @@
             def _():
                 mat_copy(d, d ^ 1, level).start()
 
-    prepare(diag_ref, face_ref, prolong_ref, sweep_w, rest_w, inv_w, restrict_w, prolong_w)
-    source = jnp.concatenate([rhs_ref[...], rhs_ref[...]], axis=0)
+    moved[3].wait()
+    source = jnp.concatenate([rhs_box[...], rhs_box[...]], axis=0)
     total = None
     for piece in three(source):
         part = lax.dot_general(order[...], piece, (((1,), (1,)), ((), ())), preferred_element_type=f32)
@@ -398,27 +421,20 @@
         tiles = own_tiles(value, level)
         if raw:
             out_face[slot, 0, :8] = value
-        else:
-            for d in first:
-                for layer in range(layers):
-                    out_face[slot, d, layer * rows:layer * rows + rows] = pack_face(
-                        tiles, level, d // 2, 1 - d % 2, layer + 1)
-                @pl.when(sides[d][0])
-                def _():
-                    face_copy(d, d ^ 1, slot, layers * rows, raw).start()
-            if deep:
-                for e in first_edges:
-                    out_edge[slot, e] = pack_edge(tiles, level, *EDGES[e])
-        if raw:
-            for d in first:
-                @pl.when(sides[d][0])
-                def _():
-                    face_copy(d, d ^ 1, slot, layers * rows, raw).start()
         if deep:
             for e in first_edges:
+                if not raw:
+                    out_edge[slot, e] = pack_edge(tiles, level, *EDGES[e])
                 @pl.when(corners[e][0])
                 def _():
                     edge_copy(e, e ^ 3, slot, raw).start()
+        for d in first:
+            for layer in range(0 if raw else layers):
+                out_face[slot, d, layer * rows:layer * rows + rows] = pack_face(
+                    tiles, level, d // 2, 1 - d % 2, layer + 1)
+            @pl.when(sides[d][0])
+            def _():
+                face_copy(d, d ^ 1, slot, layers * rows, raw).start()
         u = split(value)
         if level == 0:
             for d in range(6):
@@ -579,12 +595,20 @@
         v0[...] = v0[...] + finer(v1[...])
         double_step(0, base + 4, False, "sweep")
 
-    result = jnp.transpose(v0[...])[:MODES]
-    total = None
-    for piece in three(result):
-        part = jnp.dot(piece, order[...], preferred_element_type=f32)
-        total = part if total is None else total + part
-    out_ref[...] = total
+    pieces = three(jnp.transpose(v0[...])[:MODES])
+    back = []
+    for half in range(2):
+        columns = pl.ds(256 * half, 256)
+        total = None
+        for piece in pieces:
+            part = jnp.dot(piece, order[:, columns], preferred_element_type=f32)
+            total = part if total is None else total + part
+        result[half] = total
+        back.append(remote(
+            result.at[half], out_ref.at[:, columns], send_block.at[4 + half], recv_block.at[4 + half], owner))
+        back[half].start()
+    for copy in back:
+        copy.wait()
 
 
 def per_device(sizes, right_side, diag_blocks, face_blocks, prolong, mats_fine, mats_mid, mats_coarse):
@@ -616,6 +640,13 @@
         ] + [pltpu.SemaphoreType.DMA((SLOTS, n)) for n in (6, 6, 12, 12)] + [
             pltpu.SemaphoreType.DMA((3, 6)),
             pltpu.SemaphoreType.DMA((3, 6)),
+            vmem((64, 512)),
+            vmem((1, 512), jnp.int32),
+            vmem((1, 64), jnp.int32),
+            vmem((1, 8), jnp.int32),
+            vmem((2, 64, 256)),
+            pltpu.SemaphoreType.DMA((6,)),
+            pltpu.SemaphoreType.DMA((6,)),
         ],
         compiler_params=pltpu.CompilerParams(collective_id=0, has_side_effects=True),
         name="cycles",

time: 141 us -> 125 us (0.89)
  the two profiles are of different devices: /device:TPU:12 before, /device:TPU:39 now
where the time goes in v3:
time: 125 us
  Pallas kernels  123 us (98%)
  local copies, waits for them, and re-layouts  1.57 us (1%)
    pallas_call x1, Pallas kernels, per_device(): pl.pallas_call(partial(kernel, sizes), out_shape=jax.ShapeDtypeStruct((MO...  123 us

profile of v3, /device:TPU:39, one launch (start us, length us, event | category | flops | bytes accessed | tf_op | source)
XLA Modules:
  0.0 124.9 jit_solution(12485828284445250329)
XLA Ops:
  0.0 123.3 %cycles.1 = f32[64,512]{1,0:T(8,128)} custom-call(f32[64,512]{1,0:T(8,128)} %bitcast.6, f32[4,64,64]{2,1,0:T(8,128)} %diag_ref.1, f32[6,4,64,64]{3,2,1,0:T(8,128)} %face_ref.1, f32[8,64,64]{2,1,0:T(8,128)} %prolong_ref.1, s32[1,512]{1,0:T(1,128)} %bitcast.7, s32[1,64]{1,0:T(1,128)} %bitcast.8, s32[1,8]{1,0:T(1,128)} %bitcast.9), custom_call_target="tpu_custom_call" | custom-call | tf_op jit(solution)/shard_map/cycles/pallas_call | solution.py:620
  123.3 1.6 %copy.9 = f32[1,1,1,64,512]{4,3,2,1,0:T(8,128)} copy(f32[1,1,1,64,512]{4,3,2,1,0:T(8,128)} %bitcast.5) | data formatting | bytes 262144

commit v4 on v3

--- a/solution.py
+++ b/solution.py
@@ -298,7 +298,7 @@
     halo_g0, halo_g1, halo_g2, halo_m0, halo_m1, halo_m2,
     out_face, in_face, out_edge, in_edge, out_mat, in_mat,
     send_face, recv_face, send_edge, recv_edge, send_mat, recv_mat,
-    rhs_box, fine_box, mid_box, coarse_box, result, send_block, recv_block,
+    rhs_box, fine_box, mid_box, coarse_box, result, send_block, recv_block, inner,
 ):
     home = tuple(lax.axis_index(axis) for axis in AXES)
     run = sizes[1] // sizes[2]
@@ -412,7 +412,7 @@
         below = unpack_face(read(2 * dim + 1), level, dim, 0, layer)
         return jnp.where(bit_is(dim, 1), above, below)
 
-    def exchange(level, step, deep):
+    def exchange(level, step, deep, weights):
         slot = lax.rem(step, SLOTS)
         rows = FACE_ROWS[level]
         raw = level == 2
@@ -421,17 +421,18 @@
         tiles = own_tiles(value, level)
         if raw:
             out_face[slot, 0, :8] = value
-        if deep:
-            for e in first_edges:
-                if not raw:
-                    out_edge[slot, e] = pack_edge(tiles, level, *EDGES[e])
-                @pl.when(corners[e][0])
-                def _():
-                    edge_copy(e, e ^ 3, slot, raw).start()
+        if not raw:
+            for e in first_edges if deep else ():
+                out_edge[slot, e] = pack_edge(tiles, level, *EDGES[e])
+            for d in first:
+                for layer in range(layers):
+                    out_face[slot, d, layer * rows:layer * rows + rows] = pack_face(
+                        tiles, level, d // 2, 1 - d % 2, layer + 1)
+        for e in first_edges if deep else ():
+            @pl.when(corners[e][0])
+            def _():
+                edge_copy(e, e ^ 3, slot, raw).start()
         for d in first:
-            for layer in range(0 if raw else layers):
-                out_face[slot, d, layer * rows:layer * rows + rows] = pack_face(
-                    tiles, level, d // 2, 1 - d % 2, layer + 1)
             @pl.when(sides[d][0])
             def _():
                 face_copy(d, d ^ 1, slot, layers * rows, raw).start()
@@ -440,6 +441,20 @@
             for d in range(6):
                 place_inner(lhs, u, d)
             lhs[6] = u.reshape(2, 2, 2, 2, 2, 16, 128).astype(bf16)
+            for d in range(6):
+                place_border(lhs, u, d, jnp.zeros((16, 8, 128), f32))
+            fields = [lhs[d].reshape(512, 128) for d in range(weights.shape[0] // 256)]
+            product = twice(jnp.concatenate(fields, axis=1), weights)
+            inner[...] = chosen(product, m0[...]).reshape(inner.shape)
+        for d in range(6):
+            @pl.when(sides[d][0])
+            def _():
+                face_copy(d, d ^ 1, slot, layers * rows, raw).wait_send()
+        if deep:
+            for e in range(12):
+                @pl.when(corners[e][0])
+                def _():
+                    edge_copy(e, e ^ 3, slot, raw).wait_send()
         for d in range(6):
             @pl.when(sides[d][0])
             def _():
@@ -464,15 +479,6 @@
                 ]
                 got = [jnp.where(bit_is(q, 1), got[1], got[0]), jnp.where(bit_is(q, 1), got[3], got[2])]
                 edges.append(split_tiles(jnp.where(bit_is(p, 1), got[1], got[0])))
-        for d in range(6):
-            @pl.when(sides[d][0])
-            def _():
-                face_copy(d, d ^ 1, slot, layers * rows, raw).wait_send()
-        if deep:
-            for e in range(12):
-                @pl.when(corners[e][0])
-                def _():
-                    edge_copy(e, e ^ 3, slot, raw).wait_send()
         return u, near, far, edges
 
     def gathered(level, u, planes):
@@ -490,6 +496,23 @@
             fields = [jnp.concatenate([field, field], axis=0) for field in fields]
         return [field.astype(bf16) for field in fields]
 
+    def with_halo(planes, weights):
+        half = weights.shape[0] // 2
+        material = own_tiles(m0[...], 0)
+        for dim in range(3):
+            upper = bit_is(dim, 1)
+            both = [jnp.where(upper, planes[dim], 0.0), jnp.where(upper, 0.0, planes[dim])]
+            both = jnp.concatenate([part.reshape(-1, 128) for part in both], axis=1).astype(bf16)
+            at = 2 * dim * 128
+            w = jnp.concatenate([weights[at:at + 256], weights[half + at:half + at + 256]], axis=0)
+            product = jnp.dot(jnp.concatenate([both, both], axis=1), w, preferred_element_type=f32)
+            rows = jnp.where(upper, outer(material, 0, dim, 1, 1), outer(material, 0, dim, 0, 1))
+            term = chosen(product, rows.reshape(-1, 128)).reshape(2, 2, 2, 2, 8, 128)
+            high, low = index_at(0, dim, 1, 1), index_at(0, dim, 0, 0)
+            inner[high] = inner[high] + jnp.where(upper, term, 0.0)
+            inner[low] = inner[low] + jnp.where(upper, 0.0, term)
+        return inner[...].reshape(512, 128)
+
     def relaxed(level, value, u, planes):
         v, g, m = state[level]
         product = twice(jnp.concatenate(gathered(level, u, planes)[:6], axis=1), sweep_w)
@@ -508,7 +531,7 @@
     def double_step(level, step, fresh, last):
         v = state[level][0]
         halo_g, halo_m = halos[level]
-        u, near, far, edges = exchange(level, step, True)
+        u, near, far, edges = exchange(level, step, True, sweep_w)
         planes = [split_tiles(tiles) for tiles in near]
         raw = jnp.concatenate([tiles.reshape(-1, 128) for tiles in near], axis=0)
         if fresh:
@@ -518,7 +541,10 @@
         count = rows.shape[0]
         if count % 16:
             rows = jnp.concatenate([rows, rows[:16 - count % 16]], axis=0)
-        value = relaxed(level, v[...], u, planes)
+        if level == 0:
+            value = (1.0 - WEIGHT) * v[...] + g0[...] + with_halo(planes, sweep_w)
+        else:
+            value = relaxed(level, v[...], u, planes)
         product = twice(rows.astype(bf16), sweep_w)[:count]
         raw = (1.0 - WEIGHT) * raw + halo_g[...] + chosen(product, halo_m[...])
         planes = split(raw).reshape(3, -1, 8, 128)
@@ -534,8 +560,10 @@
 
     def single_step(level, step, last):
         v = state[level][0]
-        u, near, far, edges = exchange(level, step, False)
+        u, near, far, edges = exchange(level, step, False, sweep_w if last == "sweep" else rest_w)
         planes = [split_tiles(tiles) for tiles in near]
+        if level == 0:
+            return f0[...] - with_halo(planes, rest_w)
         if last == "sweep":
             v[...] = relaxed(level, v[...], u, planes)
             return None
@@ -647,6 +675,7 @@
             vmem((2, 64, 256)),
             pltpu.SemaphoreType.DMA((6,)),
             pltpu.SemaphoreType.DMA((6,)),
+            vmem((2, 2, 2, 2, 2, 2, 8, 128)),
         ],
         compiler_params=pltpu.CompilerParams(collective_id=0, has_side_effects=True),
         name="cycles",

time: 125 us -> 124 us (level)
  no operation moved by 1% of the time
where the time goes in v4:
time: 124 us
  Pallas kernels  122 us (98%)
  local copies, waits for them, and re-layouts  1.57 us (1%)
    pallas_call x1, Pallas kernels, per_device(): pl.pallas_call(partial(kernel, sizes), out_shape=jax.ShapeDtypeStruct((MO...  122 us

profile of v4, /device:TPU:39, one launch (start us, length us, event | category | flops | bytes accessed | tf_op | source)
XLA Modules:
  0.0 123.8 jit_solution(13232226150345544709)
XLA Ops:
  0.0 122.2 %cycles.1 = f32[64,512]{1,0:T(8,128)} custom-call(f32[64,512]{1,0:T(8,128)} %bitcast.6, f32[4,64,64]{2,1,0:T(8,128)} %diag_ref.1, f32[6,4,64,64]{3,2,1,0:T(8,128)} %face_ref.1, f32[8,64,64]{2,1,0:T(8,128)} %prolong_ref.1, s32[1,512]{1,0:T(1,128)} %bitcast.7, s32[1,64]{1,0:T(1,128)} %bitcast.8, s32[1,8]{1,0:T(1,128)} %bitcast.9), custom_call_target="tpu_custom_call" | custom-call | tf_op jit(solution)/shard_map/cycles/pallas_call | solution.py:648
  122.3 1.6 %copy.9 = f32[1,1,1,64,512]{4,3,2,1,0:T(8,128)} copy(f32[1,1,1,64,512]{4,3,2,1,0:T(8,128)} %bitcast.5) | data formatting | bytes 262144

commit v5 on v4

--- a/solution.py
+++ b/solution.py
@@ -648,7 +648,7 @@
     result = pl.pallas_call(
         partial(kernel, sizes),
         out_shape=jax.ShapeDtypeStruct((MODES, 512), f32),
-        in_specs=[pl.BlockSpec(memory_space=pltpu.VMEM)] * 7,
+        in_specs=[pl.BlockSpec(memory_space=pl.ANY)] + [pl.BlockSpec(memory_space=pltpu.VMEM)] * 6,
         out_specs=pl.BlockSpec(memory_space=pltpu.VMEM),
         scratch_shapes=[
             vmem((2 * 768, 256), bf16),

time: 124 us -> 124 us (level)
  no operation moved by 1% of the time
where the time goes in v5:
time: 124 us
  Pallas kernels  122 us (98%)
  local copies, waits for them, and re-layouts  1.57 us (1%)
    pallas_call x1, Pallas kernels, per_device(): pl.pallas_call(partial(kernel, sizes), out_shape=jax.ShapeDtypeStruct((MO...  122 us

profile of v5, /device:TPU:39, one launch (start us, length us, event | category | flops | bytes accessed | tf_op | source)
XLA Modules:
  0.0 124.0 jit_solution(7448952635017327760)
XLA Ops:
  0.0 122.4 %cycles.1 = f32[64,512]{1,0:T(8,128)} custom-call(f32[64,512]{1,0:T(8,128)} %bitcast.6, f32[4,64,64]{2,1,0:T(8,128)} %diag_ref.1, f32[6,4,64,64]{3,2,1,0:T(8,128)} %face_ref.1, f32[8,64,64]{2,1,0:T(8,128)} %prolong_ref.1, s32[1,512]{1,0:T(1,128)} %bitcast.7, s32[1,64]{1,0:T(1,128)} %bitcast.8, s32[1,8]{1,0:T(1,128)} %bitcast.9), custom_call_target="tpu_custom_call" | custom-call | tf_op jit(solution)/shard_map/cycles/pallas_call | solution.py:648
  122.4 1.6 %copy.9 = f32[1,1,1,64,512]{4,3,2,1,0:T(8,128)} copy(f32[1,1,1,64,512]{4,3,2,1,0:T(8,128)} %bitcast.5) | data formatting | bytes 262144
